TPU v7x, 256 devices: a whole 4x4x8 slice. The times are simulated.
256 devices in a mesh: gx: 64 (over z, y_lo, x), gy: 4 (over y_hi, core).
Axes of the slice: x: 4, y: 4 (y_hi: 2, y_lo: 2; y = y_hi * 2 + y_lo), z: 8, core: 2. Of those that a mesh axis runs over, the one named last changes fastest.
Arguments:
- misfit: float32 [3, 512, 128, 128], P(None, 'gx', 'gy'), may hold values from -13 to 13
- damage: float32 [512, 128, 128], P('gx', 'gy'), may hold values from 0 to 0.9
- displacement: float32 [3, 512, 128, 128], P(None, 'gx', 'gy'), may hold values from -3 to 3
Outputs:
- adjoint: float32 [3, 512, 128, 128], P(None, 'gx', 'gy')
- sensitivity: float32 [512, 128, 128], P('gx', 'gy')
All inputs are finite; a program needn't handle non-finite values.
Results may differ from a plain program's by a relative error of at most 0.00012.
Values sent between devices are 32-bit elements; how exact they have to be, the bound alone decides.
No kernel may reach another device: no remote copies, remote signals or barrier semaphores. Data moves between devices by JAX's collectives and lax.ppermute only.
A program may use at most 64 MiB of HBM per device.

v0:
```python
import math
import jax
import jax.numpy as jnp
import numpy as np
from jax import lax
from jax.sharding import Mesh
from jax.sharding import PartitionSpec as P

ITERS = 3
GX = ("gx_0", "gx_1", "gx_2")
GY = ("gy_0", "gy_1")
GX_GY = ("gx_0", "gx_1", "gx_2", "gy_0", "gy_1")


def passed_along(x, axis, by):
    devices = lax.axis_size(axis)
    pairs = [(i, i + by) for i in range(devices) if 0 <= i + by < devices]
    return lax.ppermute(x, axis, pairs)


def over_axes(x, axes):
    for axis in axes:
        x = lax.psum(x, axis)
    return x


def kronecker(first, second):
    return 1.0 if first == second else 0.0


def element_matrix():
    modulus = 3.0
    poisson_ratio = 0.3
    lame_first = modulus * poisson_ratio / ((1.0 + poisson_ratio) * (1.0 - 2.0 * poisson_ratio))
    shear_modulus = modulus / (2.0 * (1.0 + poisson_ratio))
    signs = [
        [
            2.0 * (corner_index >> 2 & 1) - 1.0,
            2.0 * (corner_index >> 1 & 1) - 1.0,
            2.0 * (corner_index & 1) - 1.0,
        ]
        for corner_index in range(8)
    ]
    elastic = [
        [
            [
                [
                    lame_first * kronecker(i, j) * kronecker(k, l)
                    + shear_modulus
                    * (kronecker(i, k) * kronecker(j, l) + kronecker(i, l) * kronecker(j, k))
                    for l in range(3)
                ]
                for k in range(3)
            ]
            for j in range(3)
        ]
        for i in range(3)
    ]
    stiffness = np.zeros((8, 3, 8, 3))
    root_three = math.sqrt(3.0)
    for gauss_index in range(8):
        gauss_point = [signs[gauss_index][dimension] / root_three for dimension in range(3)]
        gradients = [[0.0, 0.0, 0.0] for corner_index in range(8)]
        for corner_index in range(8):
            for dimension in range(3):
                factor = 0.25 * signs[corner_index][dimension]
                for others in range(3):
                    if others != dimension:
                        factor = factor * (1.0 + signs[corner_index][others] * gauss_point[others])
                gradients[corner_index][dimension] = factor
        for first_corner in range(8):
            for i in range(3):
                for second_corner in range(8):
                    for j in range(3):
                        accumulated = 0.0
                        for k in range(3):
                            for l in range(3):
                                accumulated = (
                                    accumulated
                                    + gradients[first_corner][k]
                                    * elastic[i][k][j][l]
                                    * gradients[second_corner][l]
                                )
                        stiffness[first_corner, i, second_corner, j] = (
                            stiffness[first_corner, i, second_corner, j] + 0.125 * accumulated
                        )
    return stiffness.reshape(24, 24)


def corner_offsets():
    return [
        (corner_index >> 2 & 1, corner_index >> 1 & 1, corner_index & 1)
        for corner_index in range(8)
    ]


def corner_stack(padded, count_x, count_y, count_z):
    return jnp.stack(
        [
            padded[
                :,
                shift_x : shift_x + count_x,
                shift_y : shift_y + count_y,
                shift_z : shift_z + count_z,
            ]
            for shift_x, shift_y, shift_z in corner_offsets()
        ],
        0,
    )


def element_forces(padded, degradation):
    count_x, count_y, count_z = degradation.shape
    stacked = corner_stack(padded, count_x, count_y, count_z).reshape(24, -1)
    table = jnp.asarray(element_matrix(), jnp.float32)
    forces = jnp.dot(
        table, stacked, precision=lax.Precision.HIGHEST, preferred_element_type=jnp.float32
    )
    return forces.reshape(8, 3, count_x, count_y, count_z) * degradation


def assemble(forces):
    total = None
    for corner_index, (shift_x, shift_y, shift_z) in enumerate(corner_offsets()):
        placed = jnp.pad(
            forces[corner_index],
            ((0, 0), (shift_x, 1 - shift_x), (shift_y, 1 - shift_y), (shift_z, 1 - shift_z)),
        )
        total = placed if total is None else total + placed
    return total


def apply_owned(field, degradation):
    rim_x = passed_along(field[:, :1], GX, -1)
    extended = jnp.concatenate([field, rim_x], 1)
    rim_y = passed_along(extended[:, :, :1], GY, -1)
    extended = jnp.concatenate([extended, rim_y], 2)
    extended = jnp.pad(extended, ((0, 0), (0, 0), (0, 0), (0, 1)))
    nodes = assemble(element_forces(extended, degradation))[:, :, :, :-1]
    spill_y = passed_along(nodes[:, :, -1:], GY, 1)
    nodes = jnp.concatenate([nodes[:, :, :1] + spill_y, nodes[:, :, 1:-1]], 2)
    spill_x = passed_along(nodes[:, -1:], GX, 1)
    return jnp.concatenate([nodes[:, :1] + spill_x, nodes[:, 1:-1]], 1)


def two_products(residual, image):
    return (
        over_axes(jnp.sum(residual * residual), GX_GY),
        over_axes(jnp.sum(residual * image), GX_GY),
    )


def body(misfit, damage, displacement):
    degradation = (1.0 - damage) * (1.0 - damage) + 0.001

    def operate(field):
        return apply_owned(field, degradation)

    adjoint = jnp.zeros_like(misfit)
    residual = misfit
    image = operate(residual)
    norm_now, product = two_products(residual, image)
    alpha = norm_now / product
    direction = residual
    along = image
    for step in range(ITERS):
        adjoint = adjoint + alpha * direction
        residual = residual - alpha * along
        if step + 1 < ITERS:
            image = operate(residual)
            norm_next, product = two_products(residual, image)
            ratio = norm_next / norm_now
            alpha = norm_next / (product - ratio * norm_next / alpha)
            direction = residual + ratio * direction
            along = image + ratio * along
            norm_now = norm_next
    count_x, count_y, count_z = damage.shape
    paired = jnp.concatenate([adjoint, displacement], 0)
    pair_x = passed_along(paired[:, :1], GX, -1)
    paired = jnp.concatenate([paired, pair_x], 1)
    pair_y = passed_along(paired[:, :, :1], GY, -1)
    paired = jnp.concatenate([paired, pair_y], 2)
    paired = jnp.pad(paired, ((0, 0), (0, 0), (0, 0), (0, 1)))
    table = jnp.asarray(element_matrix(), jnp.float32)
    adjoint_corners = corner_stack(paired[:3], count_x, count_y, count_z).reshape(24, -1)
    moved_corners = corner_stack(paired[3:], count_x, count_y, count_z).reshape(24, -1)
    product_terms = jnp.dot(
        table, moved_corners, precision=lax.Precision.HIGHEST, preferred_element_type=jnp.float32
    )
    contraction = jnp.sum(adjoint_corners * product_terms, 0).reshape(count_x, count_y, count_z)
    sensitivity = 2.0 * (1.0 - damage) * contraction
    return (adjoint, sensitivity)


def solution(mesh):
    split = Mesh(mesh.devices.reshape(8, 2, 4, 2, 2), ("gx_0", "gx_1", "gx_2", "gy_0", "gy_1"))
    in_specs = (P(None, GX, GY, None), P(GX, GY, None), P(None, GX, GY, None))
    out_specs = (P(None, GX, GY, None), P(GX, GY, None))
    return jax.shard_map(body, mesh=split, in_specs=in_specs, out_specs=out_specs, check_vma=False)
```

profile of v0, /device:TPU:7, one launch (start us, length us, event | category | flops | bytes accessed | tf_op | source)
XLA Modules:
  0.0 310.1 jit_solution(6029709115871913308)
XLA Ops:
  1.4 2.4 collective-permute-start
  3.9 1.8 bitcast_dynamic-update-slice_fusion.4
  5.6 1.0 constant_dynamic-update-slice_fusion.1
  6.7 1.7 collective-permute-done
  8.4 3.7 %collective-permute-start.1 = (f32[3,9,1,128]{3,2,1,0:T(1,128)S(1)}, f32[3,9,1,128]{3,2,1,0:T(1,128)S(1)}, u32[]{:S(2)}, u32[]{:S(2)}) collective-permute-start(f32[3,9,1,128]{3,2,1,0:T(1,128)S(1)} %slice.407), channel_id=1, source_target_pairs={{1,0},{2,1},{3,2},{5,4},{6,5},{7,6},{9,8},{10,9},{11,10},{13,12},{... | collective-permute-start | bytes 41480 | tf_op jit(solution)/shard_map/ppermute | solution.py:18
  13.1 3.3 %collective-permute-done.1 = f32[3,9,1,128]{3,2,1,0:T(1,128)S(1)} collective-permute-done((f32[3,9,1,128]{3,2,1,0:T(1,128)S(1)}, f32[3,9,1,128]{3,2,1,0:T(1,128)S(1)}, u32[]{:S(2)}, u32[]{:S(2)}) %collective-permute-start.1) | collective-permute-done | bytes 13856 | tf_op jit(solution)/shard_map/ppermute | solution.py:18
  18.1 0.9 fusion.10
  19.8 0.9 fusion.12
  22.4 2.9 reshape.32
  25.4 2.8 convolution_bitcast_fusion.2
  29.6 1.0 pad_add_fusion.2
  30.6 1.9 collective-permute-start.2
  32.6 1.1 collective-permute-done.2
  33.8 1.9 collective-permute-start.3
  35.7 2.9 collective-permute-done.3
  39.4 16.9 %all-reduce.30 = (f32[]{:T(128)}, f32[]{:T(128)}) all-reduce(f32[]{:T(128)} %get-tuple-element.7, f32[]{:T(128)} %get-tuple-element.6), channel_id=1, replica_groups=mesh['gx_0'=8,'gx_1'=2,'gx_2'=4,'gy_0'=2,'gy_1'=2] {'gx_0'}, use_global_device_ids=true, to_apply=%region_1.2 | all-reduce | flops 2 | bytes 16 | tf_op jit(solution)/shard_map/psum | solution.py:23
  56.3 4.6 %all-reduce.42 = (f32[]{:T(128)}, f32[]{:T(128)}) all-reduce(f32[]{:T(128)} %get-tuple-element.12, f32[]{:T(128)} %get-tuple-element.13), channel_id=1, replica_groups=mesh['gx_0'=8,'gx_1'=2,'gx_2'=4,'gy_0'=2,'gy_1'=2] {'gx_1'}, use_global_device_ids=true, to_apply=%region_2.3 | all-reduce | flops 2 | bytes 16 | tf_op jit(solution)/shard_map/psum | solution.py:23
  60.9 9.1 %all-reduce.33 = (f32[]{:T(128)}, f32[]{:T(128)}) all-reduce(f32[]{:T(128)} %get-tuple-element.36, f32[]{:T(128)} %get-tuple-element.37), channel_id=1, replica_groups=mesh['gx_0'=8,'gx_1'=2,'gx_2'=4,'gy_0'=2,'gy_1'=2] {'gx_2'}, use_global_device_ids=true, to_apply=%region_3.4 | all-reduce | flops 2 | bytes 16 | tf_op jit(solution)/shard_map/psum | solution.py:23
  70.0 5.9 %all-reduce.39 = (f32[]{:T(128)}, f32[]{:T(128)}) all-reduce(f32[]{:T(128)} %get-tuple-element.18, f32[]{:T(128)} %get-tuple-element.19), channel_id=1, replica_groups=mesh['gx_0'=8,'gx_1'=2,'gx_2'=4,'gy_0'=2,'gy_1'=2] {'gy_0'}, use_global_device_ids=true, to_apply=%region_4.5 | all-reduce | flops 2 | bytes 16 | tf_op jit(solution)/shard_map/psum | solution.py:23
  75.9 12.1 %all-reduce.36 = (f32[]{:T(128)}, f32[]{:T(128)}) all-reduce(f32[]{:T(128)} %get-tuple-element.30, f32[]{:T(128)} %get-tuple-element.31), channel_id=1, replica_groups=mesh['gx_0'=8,'gx_1'=2,'gx_2'=4,'gy_0'=2,'gy_1'=2] {'gy_1'}, use_global_device_ids=true, to_apply=%region_5.6 | all-reduce | flops 2 | bytes 16 | tf_op jit(solution)/shard_map/psum | solution.py:23
  90.2 1.9 collective-permute-start.4
  92.1 5.0 %collective-permute-done.4 = f32[3,1,32,128]{3,2,1,0:T(8,128)S(1)} collective-permute-done((f32[3,1,32,128]{3,2,1,0:T(8,128)S(1)}, f32[3,1,32,128]{3,2,1,0:T(8,128)S(1)}, u32[]{:S(2)}, u32[]{:S(2)}) %collective-permute-start.4) | collective-permute-done | bytes 49184 | tf_op jit(solution)/shard_map/ppermute | solution.py:18
  97.2 3.6 %collective-permute-start.5 = (f32[3,9,1,128]{3,2,1,0:T(1,128)S(1)}, f32[3,9,1,128]{3,2,1,0:T(1,128)S(1)}, u32[]{:S(2)}, u32[]{:S(2)}) collective-permute-start(f32[3,9,1,128]{3,2,1,0:T(1,128)S(1)} %pad_maximum_fusion.14), channel_id=1, source_target_pairs={{1,0},{2,1},{3,2},{5,4},{6,5},{7,6},{9,8},{10,9},{11,10},{13,12},{... | collective-permute-start | bytes 41480 | tf_op jit(solution)/shard_map/ppermute | solution.py:18
  100.8 4.3 %collective-permute-done.5 = f32[3,9,1,128]{3,2,1,0:T(1,128)S(1)} collective-permute-done((f32[3,9,1,128]{3,2,1,0:T(1,128)S(1)}, f32[3,9,1,128]{3,2,1,0:T(1,128)S(1)}, u32[]{:S(2)}, u32[]{:S(2)}) %collective-permute-start.5) | collective-permute-done | bytes 13856 | tf_op jit(solution)/shard_map/ppermute | solution.py:18
  106.9 0.9 fusion.18
  111.2 4.6 %reshape.34 = f32[24,32768]{1,0:T(8,128)} reshape(f32[8,3,8,32,128]{4,3,2,1,0:T(8,128)} %fusion.22) | data formatting | bytes 6291456 | tf_op jit(solution)/shard_map/reshape | solution.py:114
  115.9 4.7 %convolution_bitcast_fusion.1 = f32[3,8,256,128]{3,1,2,0:T(8,128)S(1)} fusion(f32[24,24]{1,0:T(8,128)S(1)} %copy-done.5, f32[24,32768]{1,0:T(8,128)} %reshape.34), kind=kOutput, calls=%fused_computation.10 | convolution fusion | flops 226492416 | bytes 6293760 | tf_op jit(solution)/shard_map/dot_general | solution.py:116
  122.0 1.0 pad_add_fusion.1
  123.0 1.9 collective-permute-start.6
  125.0 1.1 collective-permute-done.6
  126.1 1.9 collective-permute-start.7
  128.0 2.9 collective-permute-done.7
  131.8 11.4 %all-reduce.29 = (f32[]{:T(128)}, f32[]{:T(128)}) all-reduce(f32[]{:T(128)} %get-tuple-element.5, f32[]{:T(128)} %get-tuple-element.4), channel_id=1, replica_groups=mesh['gx_0'=8,'gx_1'=2,'gx_2'=4,'gy_0'=2,'gy_1'=2] {'gx_0'}, use_global_device_ids=true, to_apply=%region_13.14 | all-reduce | flops 2 | bytes 16 | tf_op jit(solution)/shard_map/psum | solution.py:23
  143.2 4.5 %all-reduce.41 = (f32[]{:T(128)}, f32[]{:T(128)}) all-reduce(f32[]{:T(128)} %get-tuple-element.10, f32[]{:T(128)} %get-tuple-element.11), channel_id=1, replica_groups=mesh['gx_0'=8,'gx_1'=2,'gx_2'=4,'gy_0'=2,'gy_1'=2] {'gx_1'}, use_global_device_ids=true, to_apply=%region_14.15 | all-reduce | flops 2 | bytes 16 | tf_op jit(solution)/shard_map/psum | solution.py:23
  147.6 7.9 %all-reduce.32 = (f32[]{:T(128)}, f32[]{:T(128)}) all-reduce(f32[]{:T(128)} %get-tuple-element.34, f32[]{:T(128)} %get-tuple-element.35), channel_id=1, replica_groups=mesh['gx_0'=8,'gx_1'=2,'gx_2'=4,'gy_0'=2,'gy_1'=2] {'gx_2'}, use_global_device_ids=true, to_apply=%region_15.16 | all-reduce | flops 2 | bytes 16 | tf_op jit(solution)/shard_map/psum | solution.py:23
  155.5 6.0 %all-reduce.38 = (f32[]{:T(128)}, f32[]{:T(128)}) all-reduce(f32[]{:T(128)} %get-tuple-element.16, f32[]{:T(128)} %get-tuple-element.17), channel_id=1, replica_groups=mesh['gx_0'=8,'gx_1'=2,'gx_2'=4,'gy_0'=2,'gy_1'=2] {'gy_0'}, use_global_device_ids=true, to_apply=%region_16.17 | all-reduce | flops 2 | bytes 16 | tf_op jit(solution)/shard_map/psum | solution.py:23
  161.5 12.4 %all-reduce.35 = (f32[]{:T(128)}, f32[]{:T(128)}) all-reduce(f32[]{:T(128)} %get-tuple-element.28, f32[]{:T(128)} %get-tuple-element.29), channel_id=1, replica_groups=mesh['gx_0'=8,'gx_1'=2,'gx_2'=4,'gy_0'=2,'gy_1'=2] {'gy_1'}, use_global_device_ids=true, to_apply=%region_17.18 | all-reduce | flops 2 | bytes 16 | tf_op jit(solution)/shard_map/psum | solution.py:23
  179.2 1.9 collective-permute-start.8
  181.1 5.0 %collective-permute-done.8 = f32[3,1,32,128]{3,2,1,0:T(8,128)S(1)} collective-permute-done((f32[3,1,32,128]{3,2,1,0:T(8,128)S(1)}, f32[3,1,32,128]{3,2,1,0:T(8,128)S(1)}, u32[]{:S(2)}, u32[]{:S(2)}) %collective-permute-start.8) | collective-permute-done | bytes 49184 | tf_op jit(solution)/shard_map/ppermute | solution.py:18
  186.2 3.6 %collective-permute-start.9 = (f32[3,9,1,128]{3,2,1,0:T(1,128)S(1)}, f32[3,9,1,128]{3,2,1,0:T(1,128)S(1)}, u32[]{:S(2)}, u32[]{:S(2)}) collective-permute-start(f32[3,9,1,128]{3,2,1,0:T(1,128)S(1)} %pad_maximum_fusion.13), channel_id=1, source_target_pairs={{1,0},{2,1},{3,2},{5,4},{6,5},{7,6},{9,8},{10,9},{11,10},{13,12},{... | collective-permute-start | bytes 41480 | tf_op jit(solution)/shard_map/ppermute | solution.py:18
  189.8 4.3 %collective-permute-done.9 = f32[3,9,1,128]{3,2,1,0:T(1,128)S(1)} collective-permute-done((f32[3,9,1,128]{3,2,1,0:T(1,128)S(1)}, f32[3,9,1,128]{3,2,1,0:T(1,128)S(1)}, u32[]{:S(2)}, u32[]{:S(2)}) %collective-permute-start.9) | collective-permute-done | bytes 13856 | tf_op jit(solution)/shard_map/ppermute | solution.py:18
  195.9 0.9 fusion.26
  200.2 4.6 %reshape.36 = f32[24,32768]{1,0:T(8,128)} reshape(f32[8,3,8,32,128]{4,3,2,1,0:T(8,128)} %fusion.30) | data formatting | bytes 6291456 | tf_op jit(solution)/shard_map/reshape | solution.py:114
  204.9 4.7 %convolution_bitcast_fusion = f32[3,8,256,128]{3,1,2,0:T(8,128)S(1)} fusion(f32[24,24]{1,0:T(8,128)S(1)} %copy-done.5, f32[24,32768]{1,0:T(8,128)} %reshape.36), kind=kOutput, calls=%fused_computation.9 | convolution fusion | flops 226492416 | bytes 6293760 | tf_op jit(solution)/shard_map/dot_general | solution.py:116
  211.0 1.0 pad_add_fusion
  212.1 2.1 collective-permute-start.10
  214.2 1.1 collective-permute-done.10
  215.3 1.9 collective-permute-start.11
  217.2 2.9 collective-permute-done.11
  220.9 12.4 %all-reduce.28 = (f32[]{:T(128)}, f32[]{:T(128)}) all-reduce(f32[]{:T(128)} %get-tuple-element.3, f32[]{:T(128)} %get-tuple-element.2), channel_id=1, replica_groups=mesh['gx_0'=8,'gx_1'=2,'gx_2'=4,'gy_0'=2,'gy_1'=2] {'gx_0'}, use_global_device_ids=true, to_apply=%region_25.26 | all-reduce | flops 2 | bytes 16 | tf_op jit(solution)/shard_map/psum | solution.py:23
  233.3 4.6 %all-reduce.40 = (f32[]{:T(128)}, f32[]{:T(128)}) all-reduce(f32[]{:T(128)} %get-tuple-element.8, f32[]{:T(128)} %get-tuple-element.9), channel_id=1, replica_groups=mesh['gx_0'=8,'gx_1'=2,'gx_2'=4,'gy_0'=2,'gy_1'=2] {'gx_1'}, use_global_device_ids=true, to_apply=%region_26.27 | all-reduce | flops 2 | bytes 16 | tf_op jit(solution)/shard_map/psum | solution.py:23
  237.9 8.1 %all-reduce.31 = (f32[]{:T(128)}, f32[]{:T(128)}) all-reduce(f32[]{:T(128)} %get-tuple-element.32, f32[]{:T(128)} %get-tuple-element.33), channel_id=1, replica_groups=mesh['gx_0'=8,'gx_1'=2,'gx_2'=4,'gy_0'=2,'gy_1'=2] {'gx_2'}, use_global_device_ids=true, to_apply=%region_27.28 | all-reduce | flops 2 | bytes 16 | tf_op jit(solution)/shard_map/psum | solution.py:23
  246.0 5.9 %all-reduce.37 = (f32[]{:T(128)}, f32[]{:T(128)}) all-reduce(f32[]{:T(128)} %get-tuple-element.14, f32[]{:T(128)} %get-tuple-element.15), channel_id=1, replica_groups=mesh['gx_0'=8,'gx_1'=2,'gx_2'=4,'gy_0'=2,'gy_1'=2] {'gy_0'}, use_global_device_ids=true, to_apply=%region_28.29 | all-reduce | flops 2 | bytes 16 | tf_op jit(solution)/shard_map/psum | solution.py:23
  251.9 12.1 %all-reduce.34 = (f32[]{:T(128)}, f32[]{:T(128)}) all-reduce(f32[]{:T(128)} %get-tuple-element.26, f32[]{:T(128)} %get-tuple-element.27), channel_id=1, replica_groups=mesh['gx_0'=8,'gx_1'=2,'gx_2'=4,'gy_0'=2,'gy_1'=2] {'gy_1'}, use_global_device_ids=true, to_apply=%region_29.30 | all-reduce | flops 2 | bytes 16 | tf_op jit(solution)/shard_map/psum | solution.py:23
  268.7 1.9 collective-permute-start.12
  270.7 6.1 %collective-permute-done.12 = f32[6,1,32,128]{3,2,1,0:T(8,128)S(1)} collective-permute-done((f32[6,1,32,128]{3,2,1,0:T(8,128)S(1)}, f32[6,1,32,128]{3,2,1,0:T(8,128)S(1)}, u32[]{:S(2)}, u32[]{:S(2)}) %collective-permute-start.12) | collective-permute-done | bytes 98336 | tf_op jit(solution)/shard_map/ppermute | solution.py:18
  276.8 3.1 %collective-permute-start.13 = (f32[6,9,1,128]{3,2,1,0:T(1,128)S(1)}, f32[6,9,1,128]{3,2,1,0:T(1,128)S(1)}, u32[]{:S(2)}, u32[]{:S(2)}) collective-permute-start(f32[6,9,1,128]{3,2,1,0:T(1,128)S(1)} %pad_maximum_fusion.12), channel_id=1, source_target_pairs={{1,0},{2,1},{3,2},{5,4},{6,5},{7,6},{9,8},{10,9},{11,10},{13,12},{... | collective-permute-start | bytes 82952 | tf_op jit(solution)/shard_map/ppermute | solution.py:18
  280.7 3.9 %collective-permute-done.13 = f32[6,9,1,128]{3,2,1,0:T(1,128)S(1)} collective-permute-done((f32[6,9,1,128]{3,2,1,0:T(1,128)S(1)}, f32[6,9,1,128]{3,2,1,0:T(1,128)S(1)}, u32[]{:S(2)}, u32[]{:S(2)}) %collective-permute-start.13) | collective-permute-done | bytes 27680 | tf_op jit(solution)/shard_map/ppermute | solution.py:18
  288.1 1.2 fusion.44
  289.3 1.0 fusion.47
  290.3 1.2 fusion.46
  291.5 4.6 %reshape.39 = f32[24,32768]{1,0:T(8,128)} reshape(f32[8,3,8,32,128]{4,3,2,1,0:T(8,128)} %get-tuple-element.68) | data formatting | bytes 6291456 | tf_op jit(solution)/shard_map/reshape | solution.py:186
  299.6 4.8 %reshape.38 = f32[24,32768]{1,0:T(8,128)} reshape(f32[8,3,8,32,128]{4,3,2,1,0:T(8,128)} %fusion.38) | data formatting | bytes 6291456 | tf_op jit(solution)/shard_map/reshape | solution.py:185
  304.4 5.0 %fusion = f32[32768]{0:T(1024)S(1)} fusion(f32[24,32768]{1,0:T(8,128)} %reshape.38, f32[24,24]{1,0:T(8,128)S(1)} %copy-done.5, f32[24,32768]{1,0:T(8,128)S(1)} %copy-done.2), kind=kOutput, calls=%fused_computation.27 | convolution fusion | flops 228032512 | bytes 6424832 | tf_op jit(solution)/shard_map/dot_general | solution.py:187
  (83 shorter events, 34.5 us)
Async XLA Ops:
  1.4 6.9 %collective-permute-start = (f32[3,1,32,128]{3,2,1,0:T(8,128)S(1)}, f32[3,1,32,128]{3,2,1,0:T(8,128)S(1)}, u32[]{:S(2)}, u32[]{:S(2)}) collective-permute-start(f32[3,1,32,128]{3,2,1,0:T(8,128)S(1)} %slice.322), channel_id=1, source_target_pairs={{4,0},{8,4},{12,8},{16,12},{20,16},{24,20},{28,24},{32,28},{36,32}... | collective-permute-start | bytes 147464 | tf_op jit(solution)/shard_map/ppermute | solution.py:18
  8.4 7.9 %collective-permute-start.1 = (f32[3,9,1,128]{3,2,1,0:T(1,128)S(1)}, f32[3,9,1,128]{3,2,1,0:T(1,128)S(1)}, u32[]{:S(2)}, u32[]{:S(2)}) collective-permute-start(f32[3,9,1,128]{3,2,1,0:T(1,128)S(1)} %slice.407), channel_id=1, source_target_pairs={{1,0},{2,1},{3,2},{5,4},{6,5},{7,6},{9,8},{10,9},{11,10},{13,12},{... | collective-permute-start | bytes 41480 | tf_op jit(solution)/shard_map/ppermute | solution.py:18
  22.4 2.9 copy-start.5
  29.6 9.0 %copy-start.3 = (f32[3,8,32,128]{3,2,1,0:T(8,128)S(1)}, f32[3,8,32,128]{3,2,1,0:T(8,128)}, u32[]{:S(2)}) copy-start(f32[3,8,32,128]{3,2,1,0:T(8,128)} %param.7) | copy-start | bytes 1179652
  30.6 3.1 collective-permute-start.2
  33.8 4.8 %collective-permute-start.3 = (f32[3,1,32,128]{3,2,1,0:T(8,128)S(1)}, f32[3,1,32,128]{3,2,1,0:T(8,128)S(1)}, u32[]{:S(2)}, u32[]{:S(2)}) collective-permute-start(f32[3,1,32,128]{3,2,1,0:T(8,128)S(1)} %pad_maximum_fusion.11), channel_id=1, source_target_pairs={{0,4},{4,8},{8,12},{12,16},{16,20},{20,24},{24,28},{28,32},{32,36}... | collective-permute-start | bytes 147464 | tf_op jit(solution)/shard_map/ppermute | solution.py:18
  90.2 6.9 %collective-permute-start.4 = (f32[3,1,32,128]{3,2,1,0:T(8,128)S(1)}, f32[3,1,32,128]{3,2,1,0:T(8,128)S(1)}, u32[]{:S(2)}, u32[]{:S(2)}) collective-permute-start(f32[3,1,32,128]{3,2,1,0:T(8,128)S(1)} %slice.424), channel_id=1, source_target_pairs={{4,0},{8,4},{12,8},{16,12},{20,16},{24,20},{28,24},{32,28},{36,32}... | collective-permute-start | bytes 147464 | tf_op jit(solution)/shard_map/ppermute | solution.py:18
  97.2 7.9 %collective-permute-start.5 = (f32[3,9,1,128]{3,2,1,0:T(1,128)S(1)}, f32[3,9,1,128]{3,2,1,0:T(1,128)S(1)}, u32[]{:S(2)}, u32[]{:S(2)}) collective-permute-start(f32[3,9,1,128]{3,2,1,0:T(1,128)S(1)} %pad_maximum_fusion.14), channel_id=1, source_target_pairs={{1,0},{2,1},{3,2},{5,4},{6,5},{7,6},{9,8},{10,9},{11,10},{13,12},{... | collective-permute-start | bytes 41480 | tf_op jit(solution)/shard_map/ppermute | solution.py:18
  123.0 3.1 collective-permute-start.6
  126.1 4.8 %collective-permute-start.7 = (f32[3,1,32,128]{3,2,1,0:T(8,128)S(1)}, f32[3,1,32,128]{3,2,1,0:T(8,128)S(1)}, u32[]{:S(2)}, u32[]{:S(2)}) collective-permute-start(f32[3,1,32,128]{3,2,1,0:T(8,128)S(1)} %pad_maximum_fusion.10), channel_id=1, source_target_pairs={{0,4},{4,8},{8,12},{12,16},{16,20},{20,24},{24,28},{28,32},{32,36}... | collective-permute-start | bytes 147464 | tf_op jit(solution)/shard_map/ppermute | solution.py:18
  179.2 6.9 %collective-permute-start.8 = (f32[3,1,32,128]{3,2,1,0:T(8,128)S(1)}, f32[3,1,32,128]{3,2,1,0:T(8,128)S(1)}, u32[]{:S(2)}, u32[]{:S(2)}) collective-permute-start(f32[3,1,32,128]{3,2,1,0:T(8,128)S(1)} %slice.438), channel_id=1, source_target_pairs={{4,0},{8,4},{12,8},{16,12},{20,16},{24,20},{28,24},{32,28},{36,32}... | collective-permute-start | bytes 147464 | tf_op jit(solution)/shard_map/ppermute | solution.py:18
  186.2 7.9 %collective-permute-start.9 = (f32[3,9,1,128]{3,2,1,0:T(1,128)S(1)}, f32[3,9,1,128]{3,2,1,0:T(1,128)S(1)}, u32[]{:S(2)}, u32[]{:S(2)}) collective-permute-start(f32[3,9,1,128]{3,2,1,0:T(1,128)S(1)} %pad_maximum_fusion.13), channel_id=1, source_target_pairs={{1,0},{2,1},{3,2},{5,4},{6,5},{7,6},{9,8},{10,9},{11,10},{13,12},{... | collective-permute-start | bytes 41480 | tf_op jit(solution)/shard_map/ppermute | solution.py:18
  212.0 56.7 %copy-start = (f32[3,8,32,128]{3,2,1,0:T(8,128)S(1)}, f32[3,8,32,128]{3,2,1,0:T(8,128)}, u32[]{:S(2)}) copy-start(f32[3,8,32,128]{3,2,1,0:T(8,128)} %param.9) | copy-start | bytes 1179652
  212.1 3.2 %collective-permute-start.10 = (f32[3,9,1,128]{3,2,1,0:T(1,128)S(1)}, f32[3,9,1,128]{3,2,1,0:T(1,128)S(1)}, u32[]{:S(2)}, u32[]{:S(2)}) collective-permute-start(f32[3,9,1,128]{3,2,1,0:T(1,128)S(1)} %slice.450), channel_id=1, source_target_pairs={{0,1},{1,2},{2,3},{4,5},{5,6},{6,7},{8,9},{9,10},{10,11},{12,13},{... | collective-permute-start | bytes 41480 | tf_op jit(solution)/shard_map/ppermute | solution.py:18
  215.3 4.8 %collective-permute-start.11 = (f32[3,1,32,128]{3,2,1,0:T(8,128)S(1)}, f32[3,1,32,128]{3,2,1,0:T(8,128)S(1)}, u32[]{:S(2)}, u32[]{:S(2)}) collective-permute-start(f32[3,1,32,128]{3,2,1,0:T(8,128)S(1)} %pad_maximum_fusion.9), channel_id=1, source_target_pairs={{0,4},{4,8},{8,12},{12,16},{16,20},{20,24},{24,28},{28,32},{32,36}... | collective-permute-start | bytes 147464 | tf_op jit(solution)/shard_map/ppermute | solution.py:18
  268.7 27.4 %copy-start.1 = (f32[3,8,32,128]{3,2,1,0:T(8,128)}, f32[3,8,32,128]{3,2,1,0:T(8,128)S(1)}, u32[]{:S(2)}) copy-start(f32[3,8,32,128]{3,2,1,0:T(8,128)S(1)} %get-tuple-element.39) | copy-start | bytes 1179652
  268.7 8.0 %collective-permute-start.12 = (f32[6,1,32,128]{3,2,1,0:T(8,128)S(1)}, f32[6,1,32,128]{3,2,1,0:T(8,128)S(1)}, u32[]{:S(2)}, u32[]{:S(2)}) collective-permute-start(f32[6,1,32,128]{3,2,1,0:T(8,128)S(1)} %pad_maximum_fusion.8), channel_id=1, source_target_pairs={{4,0},{8,4},{12,8},{16,12},{20,16},{24,20},{28,24},{32,28},{36,32}... | collective-permute-start | bytes 294920 | tf_op jit(solution)/shard_map/ppermute | solution.py:18
  276.8 7.8 %collective-permute-start.13 = (f32[6,9,1,128]{3,2,1,0:T(1,128)S(1)}, f32[6,9,1,128]{3,2,1,0:T(1,128)S(1)}, u32[]{:S(2)}, u32[]{:S(2)}) collective-permute-start(f32[6,9,1,128]{3,2,1,0:T(1,128)S(1)} %pad_maximum_fusion.12), channel_id=1, source_target_pairs={{1,0},{2,1},{3,2},{5,4},{6,5},{7,6},{9,8},{10,9},{11,10},{13,12},{... | collective-permute-start | bytes 82952 | tf_op jit(solution)/shard_map/ppermute | solution.py:18
  299.6 4.8 %copy-start.2 = (f32[24,32768]{1,0:T(8,128)S(1)}, f32[24,32768]{1,0:T(8,128)}, u32[]{:S(2)}) copy-start(f32[24,32768]{1,0:T(8,128)} %reshape.39) | copy-start | bytes 9437188
  304.4 5.0 %copy-start.4 = (f32[8,32,128]{2,1,0:T(8,128)S(1)}, f32[8,32,128]{2,1,0:T(8,128)}, u32[]{:S(2)}) copy-start(f32[8,32,128]{2,1,0:T(8,128)} %param.8) | copy-start | bytes 393220
where the time goes:
time: 312 us; the launch traced here: 310 us
  blocking collectives  134 us (43%)
  local copies, waits for them, and re-layouts  52.8 us (17%)
  waiting for transfers between devices  45.5 us (15%)
  starting transfers between devices  33.9 us (11%)
  matrix products  17.1 us (5%)
  other arithmetic  16.3 us (5%)
  between operations  10.7 us (3%)
    psum x15, blocking collectives, over_axes(): x = lax.psum(x, axis)  134 us
    ppermute x14, waiting for transfers between devices, passed_along(): return lax.ppermute(x, axis, pairs)  45.5 us
    ppermute x14, starting transfers between devices, passed_along(): return lax.ppermute(x, axis, pairs)  33.9 us
    unnamed x39, local copies, waits for them, and re-layouts  24.1 us
    reshape x3, local copies, waits for them, and re-layouts, element_forces(): stacked = corner_stack(padded, count_x, count_y, count_z).reshape(24, -1)  12.2 us
    dot_general x3, matrix products, element_forces(): jnp.dot(table, stacked, precision=lax.Precision.HIGHEST, preferred_elemen...  12.1 us
    unnamed x9, other arithmetic  7.31 us
  transfers between devices with their start and end apart: 14, of which 14 were waited for; matrix products, arithmetic and copies ran while one was open for 1% of the time, Pallas kernels for 0%

commit v1 on v0

--- a/solution.py
+++ b/solution.py
@@ -20,7 +20,7 @@
 
 def over_axes(x, axes):
     for axis in axes:
-        x = lax.psum(x, axis)
+        x = jnp.sum(lax.all_gather(x, axis), axis=0)
     return x
 
 

time: 312 us -> 366 us (1.17)
  local copies, waits for them, and re-layouts: 52.8 us -> 97.6 us
  other arithmetic: 16.3 us -> 35.4 us
  blocking collectives: 134 us -> 124 us
    psum x15 -> x0, blocking collectives: 134 us -> none  [over_axes(): x = lax.psum(x, axis)]
    unnamed x0 -> x15, blocking collectives: none -> 124 us
    unnamed x39 -> x114, local copies, waits for them, and re-layouts: 24.1 us -> 69 us
    reduce_sum x0 -> x30, other arithmetic: none -> 19.1 us  [over_axes(): x = jnp.sum(lax.all_gather(x, axis), axis=0)]
where the time goes in v1:
time: 366 us; the launch traced here: 364 us
  blocking collectives  124 us (34%)
  local copies, waits for them, and re-layouts  97.6 us (27%)
  waiting for transfers between devices  44.7 us (12%)
  other arithmetic  35.4 us (10%)
  starting transfers between devices  34.2 us (9%)
  matrix products  17.1 us (5%)
  between operations  11.2 us (3%)
    unnamed x15, blocking collectives  124 us
    unnamed x114, local copies, waits for them, and re-layouts  69 us
    ppermute x14, waiting for transfers between devices, passed_along(): return lax.ppermute(x, axis, pairs)  44.7 us
    ppermute x14, starting transfers between devices, passed_along(): return lax.ppermute(x, axis, pairs)  34.2 us
    reduce_sum x30, other arithmetic, over_axes(): x = jnp.sum(lax.all_gather(x, axis), axis=0)  19.1 us
    reshape x3, local copies, waits for them, and re-layouts, element_forces(): stacked = corner_stack(padded, count_x, count_y, count_z).reshape(24, -1)  12.2 us
    dot_general x3, matrix products, element_forces(): jnp.dot(table, stacked, precision=lax.Precision.HIGHEST, preferred_elemen...  12.1 us
  transfers between devices with their start and end apart: 14, of which 14 were waited for; matrix products, arithmetic and copies ran while one was open for 1% of the time, Pallas kernels for 0%

profile of v1, /device:TPU:7, one launch (start us, length us, event | category | flops | bytes accessed | tf_op | source)
XLA Modules:
  0.0 364.0 jit_solution(4921738198780104436)
XLA Ops:
  1.4 2.4 collective-permute-start
  3.9 1.8 bitcast_dynamic-update-slice_fusion.4
  6.7 1.7 collective-permute-done
  8.4 3.7 %collective-permute-start.1 = (f32[3,9,1,128]{3,2,1,0:T(1,128)S(1)}, f32[3,9,1,128]{3,2,1,0:T(1,128)S(1)}, u32[]{:S(2)}, u32[]{:S(2)}) collective-permute-start(f32[3,9,1,128]{3,2,1,0:T(1,128)S(1)} %slice.407), channel_id=1, source_target_pairs={{1,0},{2,1},{3,2},{5,4},{6,5},{7,6},{9,8},{10,9},{11,10},{13,12},{... | collective-permute-start | bytes 41480 | tf_op jit(solution)/shard_map/ppermute | solution.py:18
  13.1 3.3 collective-permute-done.1
  22.4 2.9 reshape.32
  25.4 2.8 convolution_bitcast_fusion.2
  30.8 1.9 collective-permute-start.2
  33.9 1.9 collective-permute-start.3
  36.4 2.3 collective-permute-done.3
  42.8 16.2 %all-reduce.60 = (f32[8]{0:T(128)S(1)}, f32[8]{0:T(128)S(1)}) all-reduce(f32[8]{0:T(128)S(1)} %dynamic-update-slice, f32[8]{0:T(128)S(1)} %dynamic-update-slice.5), channel_id=1, replica_groups=mesh['gx_0'=8,'gx_1'=2,'gx_2'=4,'gy_0'=2,'gy_1'=2] {'gx_0'}, use_global_device_ids=true, to_apply=%add.28 | all-reduce | flops 16 | bytes 128
  60.3 1.4 dynamic-update-slice.6
  61.7 1.4 dynamic-update-slice.1
  63.7 3.8 %all-reduce.72 = (f32[2]{0:T(128)S(1)}, f32[2]{0:T(128)S(1)}) all-reduce(f32[2]{0:T(128)S(1)} %dynamic-update-slice.1, f32[2]{0:T(128)S(1)} %dynamic-update-slice.6), channel_id=1, replica_groups=mesh['gx_0'=8,'gx_1'=2,'gx_2'=4,'gy_0'=2,'gy_1'=2] {'gx_1'}, use_global_device_ids=true, to_apply=%add.29 | all-reduce | flops 4 | bytes 32
  68.8 1.4 dynamic-update-slice.7
  72.3 8.5 %all-reduce.63 = (f32[4]{0:T(128)S(1)}, f32[4]{0:T(128)S(1)}) all-reduce(f32[4]{0:T(128)S(1)} %dynamic-update-slice.2, f32[4]{0:T(128)S(1)} %dynamic-update-slice.7), channel_id=1, replica_groups=mesh['gx_0'=8,'gx_1'=2,'gx_2'=4,'gy_0'=2,'gy_1'=2] {'gx_2'}, use_global_device_ids=true, to_apply=%add.30 | all-reduce | flops 8 | bytes 64
  82.1 1.4 dynamic-update-slice.8
  85.5 5.3 %all-reduce.69 = (f32[2]{0:T(128)S(1)}, f32[2]{0:T(128)S(1)}) all-reduce(f32[2]{0:T(128)S(1)} %dynamic-update-slice.3, f32[2]{0:T(128)S(1)} %dynamic-update-slice.8), channel_id=1, replica_groups=mesh['gx_0'=8,'gx_1'=2,'gx_2'=4,'gy_0'=2,'gy_1'=2] {'gy_0'}, use_global_device_ids=true, to_apply=%add.31 | all-reduce | flops 4 | bytes 32
  92.0 1.4 dynamic-update-slice.9
  94.8 11.7 %all-reduce.66 = (f32[2]{0:T(128)S(1)}, f32[2]{0:T(128)S(1)}) all-reduce(f32[2]{0:T(128)S(1)} %dynamic-update-slice.4, f32[2]{0:T(128)S(1)} %dynamic-update-slice.9), channel_id=1, replica_groups=mesh['gx_0'=8,'gx_1'=2,'gx_2'=4,'gy_0'=2,'gy_1'=2] {'gy_1'}, use_global_device_ids=true, to_apply=%add.32 | all-reduce | flops 4 | bytes 32
  109.8 1.9 collective-permute-start.4
  111.8 5.0 %collective-permute-done.4 = f32[3,1,32,128]{3,2,1,0:T(8,128)S(1)} collective-permute-done((f32[3,1,32,128]{3,2,1,0:T(8,128)S(1)}, f32[3,1,32,128]{3,2,1,0:T(8,128)S(1)}, u32[]{:S(2)}, u32[]{:S(2)}) %collective-permute-start.4) | collective-permute-done | bytes 49184 | tf_op jit(solution)/shard_map/ppermute | solution.py:18
  116.8 3.6 collective-permute-start.5
  120.4 4.3 %collective-permute-done.5 = f32[3,9,1,128]{3,2,1,0:T(1,128)S(1)} collective-permute-done((f32[3,9,1,128]{3,2,1,0:T(1,128)S(1)}, f32[3,9,1,128]{3,2,1,0:T(1,128)S(1)}, u32[]{:S(2)}, u32[]{:S(2)}) %collective-permute-start.5) | collective-permute-done | bytes 13856 | tf_op jit(solution)/shard_map/ppermute | solution.py:18
  130.9 4.6 %reshape.34 = f32[24,32768]{1,0:T(8,128)} reshape(f32[8,3,8,32,128]{4,3,2,1,0:T(8,128)} %fusion.22) | data formatting | bytes 6291456 | tf_op jit(solution)/shard_map/reshape | solution.py:114
  135.5 4.7 %convolution_bitcast_fusion.1 = f32[3,8,256,128]{3,1,2,0:T(8,128)S(1)} fusion(f32[24,24]{1,0:T(8,128)S(1)} %copy-done.5, f32[24,32768]{1,0:T(8,128)} %reshape.34), kind=kOutput, calls=%fused_computation.10 | convolution fusion | flops 226492416 | bytes 6293760 | tf_op jit(solution)/shard_map/dot_general | solution.py:116
  142.6 1.9 collective-permute-start.6
  145.7 1.9 collective-permute-start.7
  147.7 2.9 collective-permute-done.7
  154.0 10.7 %all-reduce.59 = (f32[8]{0:T(128)S(1)}, f32[8]{0:T(128)S(1)}) all-reduce(f32[8]{0:T(128)S(1)} %dynamic-update-slice.10, f32[8]{0:T(128)S(1)} %dynamic-update-slice.15), channel_id=1, replica_groups=mesh['gx_0'=8,'gx_1'=2,'gx_2'=4,'gy_0'=2,'gy_1'=2] {'gx_0'}, use_global_device_ids=true, to_apply=%add.38 | all-reduce | flops 16 | bytes 128
  165.4 1.4 dynamic-update-slice.16
  167.5 1.4 dynamic-update-slice.11
  168.9 3.8 %all-reduce.71 = (f32[2]{0:T(128)S(1)}, f32[2]{0:T(128)S(1)}) all-reduce(f32[2]{0:T(128)S(1)} %dynamic-update-slice.11, f32[2]{0:T(128)S(1)} %dynamic-update-slice.16), channel_id=1, replica_groups=mesh['gx_0'=8,'gx_1'=2,'gx_2'=4,'gy_0'=2,'gy_1'=2] {'gx_1'}, use_global_device_ids=true, to_apply=%add.39 | all-reduce | flops 4 | bytes 32
  173.4 1.4 dynamic-update-slice.17
  175.5 1.4 dynamic-update-slice.12
  176.9 7.2 %all-reduce.62 = (f32[4]{0:T(128)S(1)}, f32[4]{0:T(128)S(1)}) all-reduce(f32[4]{0:T(128)S(1)} %dynamic-update-slice.12, f32[4]{0:T(128)S(1)} %dynamic-update-slice.17), channel_id=1, replica_groups=mesh['gx_0'=8,'gx_1'=2,'gx_2'=4,'gy_0'=2,'gy_1'=2] {'gx_2'}, use_global_device_ids=true, to_apply=%add.40 | all-reduce | flops 8 | bytes 64
  184.8 1.4 dynamic-update-slice.18
  186.9 1.4 dynamic-update-slice.13
  188.3 5.3 %all-reduce.68 = (f32[2]{0:T(128)S(1)}, f32[2]{0:T(128)S(1)}) all-reduce(f32[2]{0:T(128)S(1)} %dynamic-update-slice.13, f32[2]{0:T(128)S(1)} %dynamic-update-slice.18), channel_id=1, replica_groups=mesh['gx_0'=8,'gx_1'=2,'gx_2'=4,'gy_0'=2,'gy_1'=2] {'gy_0'}, use_global_device_ids=true, to_apply=%add.41 | all-reduce | flops 4 | bytes 32
  194.3 1.4 dynamic-update-slice.19
  196.4 1.4 dynamic-update-slice.14
  197.8 11.7 %all-reduce.65 = (f32[2]{0:T(128)S(1)}, f32[2]{0:T(128)S(1)}) all-reduce(f32[2]{0:T(128)S(1)} %dynamic-update-slice.14, f32[2]{0:T(128)S(1)} %dynamic-update-slice.19), channel_id=1, replica_groups=mesh['gx_0'=8,'gx_1'=2,'gx_2'=4,'gy_0'=2,'gy_1'=2] {'gy_1'}, use_global_device_ids=true, to_apply=%add.42 | all-reduce | flops 4 | bytes 32
  216.4 1.9 collective-permute-start.8
  218.3 5.0 %collective-permute-done.8 = f32[3,1,32,128]{3,2,1,0:T(8,128)S(1)} collective-permute-done((f32[3,1,32,128]{3,2,1,0:T(8,128)S(1)}, f32[3,1,32,128]{3,2,1,0:T(8,128)S(1)}, u32[]{:S(2)}, u32[]{:S(2)}) %collective-permute-start.8) | collective-permute-done | bytes 49184 | tf_op jit(solution)/shard_map/ppermute | solution.py:18
  223.3 3.6 collective-permute-start.9
  226.9 4.3 %collective-permute-done.9 = f32[3,9,1,128]{3,2,1,0:T(1,128)S(1)} collective-permute-done((f32[3,9,1,128]{3,2,1,0:T(1,128)S(1)}, f32[3,9,1,128]{3,2,1,0:T(1,128)S(1)}, u32[]{:S(2)}, u32[]{:S(2)}) %collective-permute-start.9) | collective-permute-done | bytes 13856 | tf_op jit(solution)/shard_map/ppermute | solution.py:18
  237.4 4.6 %reshape.36 = f32[24,32768]{1,0:T(8,128)} reshape(f32[8,3,8,32,128]{4,3,2,1,0:T(8,128)} %fusion.30) | data formatting | bytes 6291456 | tf_op jit(solution)/shard_map/reshape | solution.py:114
  242.0 4.7 %convolution_bitcast_fusion = f32[3,8,256,128]{3,1,2,0:T(8,128)S(1)} fusion(f32[24,24]{1,0:T(8,128)S(1)} %copy-done.5, f32[24,32768]{1,0:T(8,128)} %reshape.36), kind=kOutput, calls=%fused_computation.9 | convolution fusion | flops 226492416 | bytes 6293760 | tf_op jit(solution)/shard_map/dot_general | solution.py:116
  249.2 2.1 collective-permute-start.10
  252.4 1.9 collective-permute-start.11
  254.3 2.9 collective-permute-done.11
  260.6 11.7 %all-reduce.58 = (f32[8]{0:T(128)S(1)}, f32[8]{0:T(128)S(1)}) all-reduce(f32[8]{0:T(128)S(1)} %dynamic-update-slice.20, f32[8]{0:T(128)S(1)} %dynamic-update-slice.25), channel_id=1, replica_groups=mesh['gx_0'=8,'gx_1'=2,'gx_2'=4,'gy_0'=2,'gy_1'=2] {'gx_0'}, use_global_device_ids=true, to_apply=%add.48 | all-reduce | flops 16 | bytes 128
  274.9 1.4 dynamic-update-slice.21
  276.3 3.8 %all-reduce.70 = (f32[2]{0:T(128)S(1)}, f32[2]{0:T(128)S(1)}) all-reduce(f32[2]{0:T(128)S(1)} %dynamic-update-slice.21, f32[2]{0:T(128)S(1)} %dynamic-update-slice.26), channel_id=1, replica_groups=mesh['gx_0'=8,'gx_1'=2,'gx_2'=4,'gy_0'=2,'gy_1'=2] {'gx_1'}, use_global_device_ids=true, to_apply=%add.49 | all-reduce | flops 4 | bytes 32
  284.1 7.5 %all-reduce.61 = (f32[4]{0:T(128)S(1)}, f32[4]{0:T(128)S(1)}) all-reduce(f32[4]{0:T(128)S(1)} %dynamic-update-slice.22, f32[4]{0:T(128)S(1)} %dynamic-update-slice.27), channel_id=1, replica_groups=mesh['gx_0'=8,'gx_1'=2,'gx_2'=4,'gy_0'=2,'gy_1'=2] {'gx_2'}, use_global_device_ids=true, to_apply=%add.50 | all-reduce | flops 8 | bytes 64
  295.5 5.3 %all-reduce.67 = (f32[2]{0:T(128)S(1)}, f32[2]{0:T(128)S(1)}) all-reduce(f32[2]{0:T(128)S(1)} %dynamic-update-slice.23, f32[2]{0:T(128)S(1)} %dynamic-update-slice.28), channel_id=1, replica_groups=mesh['gx_0'=8,'gx_1'=2,'gx_2'=4,'gy_0'=2,'gy_1'=2] {'gy_0'}, use_global_device_ids=true, to_apply=%add.51 | all-reduce | flops 4 | bytes 32
  304.8 11.7 %all-reduce.64 = (f32[2]{0:T(128)S(1)}, f32[2]{0:T(128)S(1)}) all-reduce(f32[2]{0:T(128)S(1)} %dynamic-update-slice.24, f32[2]{0:T(128)S(1)} %dynamic-update-slice.29), channel_id=1, replica_groups=mesh['gx_0'=8,'gx_1'=2,'gx_2'=4,'gy_0'=2,'gy_1'=2] {'gy_1'}, use_global_device_ids=true, to_apply=%add.52 | all-reduce | flops 4 | bytes 32
  322.6 1.9 collective-permute-start.12
  324.6 6.1 %collective-permute-done.12 = f32[6,1,32,128]{3,2,1,0:T(8,128)S(1)} collective-permute-done((f32[6,1,32,128]{3,2,1,0:T(8,128)S(1)}, f32[6,1,32,128]{3,2,1,0:T(8,128)S(1)}, u32[]{:S(2)}, u32[]{:S(2)}) %collective-permute-start.12) | collective-permute-done | bytes 98336 | tf_op jit(solution)/shard_map/ppermute | solution.py:18
  330.7 3.4 collective-permute-start.13
  334.9 3.6 collective-permute-done.13
  345.4 4.6 %reshape.39 = f32[24,32768]{1,0:T(8,128)} reshape(f32[8,3,8,32,128]{4,3,2,1,0:T(8,128)} %get-tuple-element.68) | data formatting | bytes 6291456 | tf_op jit(solution)/shard_map/reshape | solution.py:186
  353.4 4.8 %reshape.38 = f32[24,32768]{1,0:T(8,128)} reshape(f32[8,3,8,32,128]{4,3,2,1,0:T(8,128)} %fusion.38) | data formatting | bytes 6291456 | tf_op jit(solution)/shard_map/reshape | solution.py:185
  358.3 5.0 %fusion = f32[32768]{0:T(1024)S(1)} fusion(f32[24,32768]{1,0:T(8,128)} %reshape.38, f32[24,24]{1,0:T(8,128)S(1)} %copy-done.5, f32[24,32768]{1,0:T(8,128)S(1)} %copy-done.2), kind=kOutput, calls=%fused_computation.27 | convolution fusion | flops 228032512 | bytes 6424832 | tf_op jit(solution)/shard_map/dot_general | solution.py:187
  (188 shorter events, 92.8 us)
Async XLA Ops:
  1.4 6.9 %collective-permute-start = (f32[3,1,32,128]{3,2,1,0:T(8,128)S(1)}, f32[3,1,32,128]{3,2,1,0:T(8,128)S(1)}, u32[]{:S(2)}, u32[]{:S(2)}) collective-permute-start(f32[3,1,32,128]{3,2,1,0:T(8,128)S(1)} %slice.322), channel_id=1, source_target_pairs={{4,0},{8,4},{12,8},{16,12},{20,16},{24,20},{28,24},{32,28},{36,32}... | collective-permute-start | bytes 147464 | tf_op jit(solution)/shard_map/ppermute | solution.py:18
  8.4 7.9 %collective-permute-start.1 = (f32[3,9,1,128]{3,2,1,0:T(1,128)S(1)}, f32[3,9,1,128]{3,2,1,0:T(1,128)S(1)}, u32[]{:S(2)}, u32[]{:S(2)}) collective-permute-start(f32[3,9,1,128]{3,2,1,0:T(1,128)S(1)} %slice.407), channel_id=1, source_target_pairs={{1,0},{2,1},{3,2},{5,4},{6,5},{7,6},{9,8},{10,9},{11,10},{13,12},{... | collective-permute-start | bytes 41480 | tf_op jit(solution)/shard_map/ppermute | solution.py:18
  22.4 2.9 copy-start.5
  29.6 6.2 %copy-start.10 = (u32[256]{0:T(256)S(1)}, u32[256]{0:T(256)}, u32[]{:S(2)}) copy-start(u32[256]{0:T(256)} %constant.74) | copy-start | bytes 3076
  29.7 9.1 %copy-start.3 = (f32[3,8,32,128]{3,2,1,0:T(8,128)S(1)}, f32[3,8,32,128]{3,2,1,0:T(8,128)}, u32[]{:S(2)}) copy-start(f32[3,8,32,128]{3,2,1,0:T(8,128)} %param.7) | copy-start | bytes 1179652
  29.7 12.5 %copy-start.9 = (u32[256]{0:T(256)S(1)}, u32[256]{0:T(256)}, u32[]{:S(2)}) copy-start(u32[256]{0:T(256)} %constant.79) | copy-start | bytes 3076
  29.7 33.5 %copy-start.8 = (u32[256]{0:T(256)S(1)}, u32[256]{0:T(256)}, u32[]{:S(2)}) copy-start(u32[256]{0:T(256)} %constant.84) | copy-start | bytes 3076
  29.7 41.9 %copy-start.7 = (u32[256]{0:T(256)S(1)}, u32[256]{0:T(256)}, u32[]{:S(2)}) copy-start(u32[256]{0:T(256)} %constant.89) | copy-start | bytes 3076
  29.7 55.2 %copy-start.6 = (u32[256]{0:T(256)S(1)}, u32[256]{0:T(256)}, u32[]{:S(2)}) copy-start(u32[256]{0:T(256)} %constant.94) | copy-start | bytes 3076
  30.8 3.1 collective-permute-start.2
  33.9 4.8 %collective-permute-start.3 = (f32[3,1,32,128]{3,2,1,0:T(8,128)S(1)}, f32[3,1,32,128]{3,2,1,0:T(8,128)S(1)}, u32[]{:S(2)}, u32[]{:S(2)}) collective-permute-start(f32[3,1,32,128]{3,2,1,0:T(8,128)S(1)} %pad_maximum_fusion.11), channel_id=1, source_target_pairs={{0,4},{4,8},{8,12},{12,16},{16,20},{20,24},{24,28},{28,32},{32,36}... | collective-permute-start | bytes 147464 | tf_op jit(solution)/shard_map/ppermute | solution.py:18
  109.8 6.9 %collective-permute-start.4 = (f32[3,1,32,128]{3,2,1,0:T(8,128)S(1)}, f32[3,1,32,128]{3,2,1,0:T(8,128)S(1)}, u32[]{:S(2)}, u32[]{:S(2)}) collective-permute-start(f32[3,1,32,128]{3,2,1,0:T(8,128)S(1)} %slice.424), channel_id=1, source_target_pairs={{4,0},{8,4},{12,8},{16,12},{20,16},{24,20},{28,24},{32,28},{36,32}... | collective-permute-start | bytes 147464 | tf_op jit(solution)/shard_map/ppermute | solution.py:18
  116.8 7.9 %collective-permute-start.5 = (f32[3,9,1,128]{3,2,1,0:T(1,128)S(1)}, f32[3,9,1,128]{3,2,1,0:T(1,128)S(1)}, u32[]{:S(2)}, u32[]{:S(2)}) collective-permute-start(f32[3,9,1,128]{3,2,1,0:T(1,128)S(1)} %pad_maximum_fusion.14), channel_id=1, source_target_pairs={{1,0},{2,1},{3,2},{5,4},{6,5},{7,6},{9,8},{10,9},{11,10},{13,12},{... | collective-permute-start | bytes 41480 | tf_op jit(solution)/shard_map/ppermute | solution.py:18
  142.6 3.1 collective-permute-start.6
  145.7 4.8 %collective-permute-start.7 = (f32[3,1,32,128]{3,2,1,0:T(8,128)S(1)}, f32[3,1,32,128]{3,2,1,0:T(8,128)S(1)}, u32[]{:S(2)}, u32[]{:S(2)}) collective-permute-start(f32[3,1,32,128]{3,2,1,0:T(8,128)S(1)} %pad_maximum_fusion.10), channel_id=1, source_target_pairs={{0,4},{4,8},{8,12},{12,16},{16,20},{20,24},{24,28},{28,32},{32,36}... | collective-permute-start | bytes 147464 | tf_op jit(solution)/shard_map/ppermute | solution.py:18
  216.4 6.9 %collective-permute-start.8 = (f32[3,1,32,128]{3,2,1,0:T(8,128)S(1)}, f32[3,1,32,128]{3,2,1,0:T(8,128)S(1)}, u32[]{:S(2)}, u32[]{:S(2)}) collective-permute-start(f32[3,1,32,128]{3,2,1,0:T(8,128)S(1)} %slice.438), channel_id=1, source_target_pairs={{4,0},{8,4},{12,8},{16,12},{20,16},{24,20},{28,24},{32,28},{36,32}... | collective-permute-start | bytes 147464 | tf_op jit(solution)/shard_map/ppermute | solution.py:18
  223.3 7.9 %collective-permute-start.9 = (f32[3,9,1,128]{3,2,1,0:T(1,128)S(1)}, f32[3,9,1,128]{3,2,1,0:T(1,128)S(1)}, u32[]{:S(2)}, u32[]{:S(2)}) collective-permute-start(f32[3,9,1,128]{3,2,1,0:T(1,128)S(1)} %pad_maximum_fusion.13), channel_id=1, source_target_pairs={{1,0},{2,1},{3,2},{5,4},{6,5},{7,6},{9,8},{10,9},{11,10},{13,12},{... | collective-permute-start | bytes 41480 | tf_op jit(solution)/shard_map/ppermute | solution.py:18
  249.1 73.5 %copy-start = (f32[3,8,32,128]{3,2,1,0:T(8,128)S(1)}, f32[3,8,32,128]{3,2,1,0:T(8,128)}, u32[]{:S(2)}) copy-start(f32[3,8,32,128]{3,2,1,0:T(8,128)} %param.9) | copy-start | bytes 1179652
  249.2 3.2 collective-permute-start.10
  252.4 4.8 %collective-permute-start.11 = (f32[3,1,32,128]{3,2,1,0:T(8,128)S(1)}, f32[3,1,32,128]{3,2,1,0:T(8,128)S(1)}, u32[]{:S(2)}, u32[]{:S(2)}) collective-permute-start(f32[3,1,32,128]{3,2,1,0:T(8,128)S(1)} %pad_maximum_fusion.9), channel_id=1, source_target_pairs={{0,4},{4,8},{8,12},{12,16},{16,20},{20,24},{24,28},{28,32},{32,36}... | collective-permute-start | bytes 147464 | tf_op jit(solution)/shard_map/ppermute | solution.py:18
  322.6 27.4 %copy-start.1 = (f32[3,8,32,128]{3,2,1,0:T(8,128)}, f32[3,8,32,128]{3,2,1,0:T(8,128)S(1)}, u32[]{:S(2)}) copy-start(f32[3,8,32,128]{3,2,1,0:T(8,128)S(1)} %get-tuple-element.39) | copy-start | bytes 1179652
  322.6 8.0 %collective-permute-start.12 = (f32[6,1,32,128]{3,2,1,0:T(8,128)S(1)}, f32[6,1,32,128]{3,2,1,0:T(8,128)S(1)}, u32[]{:S(2)}, u32[]{:S(2)}) collective-permute-start(f32[6,1,32,128]{3,2,1,0:T(8,128)S(1)} %pad_maximum_fusion.8), channel_id=1, source_target_pairs={{4,0},{8,4},{12,8},{16,12},{20,16},{24,20},{28,24},{32,28},{36,32}... | collective-permute-start | bytes 294920 | tf_op jit(solution)/shard_map/ppermute | solution.py:18
  330.7 7.8 %collective-permute-start.13 = (f32[6,9,1,128]{3,2,1,0:T(1,128)S(1)}, f32[6,9,1,128]{3,2,1,0:T(1,128)S(1)}, u32[]{:S(2)}, u32[]{:S(2)}) collective-permute-start(f32[6,9,1,128]{3,2,1,0:T(1,128)S(1)} %pad_maximum_fusion.12), channel_id=1, source_target_pairs={{1,0},{2,1},{3,2},{5,4},{6,5},{7,6},{9,8},{10,9},{11,10},{13,12},{... | collective-permute-start | bytes 82952 | tf_op jit(solution)/shard_map/ppermute | solution.py:18
  353.4 4.8 %copy-start.2 = (f32[24,32768]{1,0:T(8,128)S(1)}, f32[24,32768]{1,0:T(8,128)}, u32[]{:S(2)}) copy-start(f32[24,32768]{1,0:T(8,128)} %reshape.39) | copy-start | bytes 9437188
  358.3 5.0 %copy-start.4 = (f32[8,32,128]{2,1,0:T(8,128)S(1)}, f32[8,32,128]{2,1,0:T(8,128)}, u32[]{:S(2)}) copy-start(f32[8,32,128]{2,1,0:T(8,128)} %param.8) | copy-start | bytes 393220
